TPU v7x, 32 devices: a whole 2x2x4 slice. The times are simulated.
32 devices in a mesh: groups: 2 (over x), span: 8 (over z, y), head: 2 (over core).
Axes of the slice: x: 2, y: 2, z: 4, core: 2. Of those that a mesh axis runs over, the one named last changes fastest.
Arguments:
- span_states: bfloat16 [2048, 4096], P(('groups', 'span'), 'head'), parts along dimension 0, may hold values from -1.5 to 1.5
- span_queries: bfloat16 [2048, 2048], P(('groups', 'span'), 'head'), parts along dimension 0, may hold values from -1000 to 1000
- span_memory: bfloat16 [2048, 2, 896], P(('groups', 'span'), None, 'head'), parts along dimension 0, may hold values from -1000 to 1000
- passages: bfloat16 [16384, 896], P(('groups', 'span')), parts along dimension 0, may hold values from -1.5 to 1.5
- neighbours: int32 [32, 2], P(('groups', 'span')), parts along dimension 0, may hold values from 0 to 63, as said below
- enc_query_w: bfloat16 [896, 896], P(None, 'head'), may hold values from -0.1875 to 0.1875
- enc_out_w: bfloat16 [896, 896], P(None, 'head'), may hold values from -0.1875 to 0.1875
- kv_weight: bfloat16 [896, 2, 2048], P(None, None, ('head', 'span')), may hold values from -0.1875 to 0.1875
- out_weight: bfloat16 [2048, 4096], P('head', 'span'), may hold values from -0.125 to 0.125
Outputs:
- mixed_states: bfloat16 [2048, 4096], P(('groups', 'span'), 'head'), parts along dimension 0
There are 2 independent parts, one for each index of `groups`. A program takes and returns all parts, laid end to end along the dimension named above; an argument that names none is the same for every part. Nothing has to cross between parts.
Inputs may be any that keep to these rules, and one draw needn't show every extreme that they name: `neighbours`: passage p belongs to index p // 8 of the span axis. Among the spans of one index of the span axis, all 4 passages listed belong to distinct indices.
All inputs are finite; a program needn't handle non-finite values.
Results may differ from a plain program's by a relative error of at most 0.025.
Values may be sent and summed in bfloat16 or wider, within the bound.
A program may use at most 64 MiB of HBM per device.

v0:
```python
import math
import jax
import jax.numpy as jnp
from jax import lax
from jax.sharding import PartitionSpec as P

HD = 128
E = 896
EHD = 64
CT = 64
PT = 128
NB = 2
PS_DEV = 8
epsilon = 1e-06


def rms_rows(values):
    return values * lax.rsqrt(jnp.mean(values * values, axis=-1, keepdims=True) + epsilon)


def softmax_rows(scores):
    top_score = jnp.max(scores, axis=-1, keepdims=True)
    raised = jnp.exp(scores - top_score)
    return raised / jnp.sum(raised, axis=-1, keepdims=True)


def wanted_slots(owner_flat, local_flat, device_count):
    matched = owner_flat[:, None] == jnp.arange(device_count, dtype=jnp.int32)[None, :]
    return jnp.sum(jnp.where(matched, local_flat[:, None], 0), axis=0)


def fetch_passages(wanted, passages):
    blocks = passages.reshape(-1, PT, E)
    picked = blocks[lax.all_to_all(wanted, "span", split_axis=0, concat_axis=0, tiled=True)]
    return lax.all_to_all(picked, "span", split_axis=0, concat_axis=0, tiled=True)


def encode_branch(copies, memory, query_w, out_w):
    groups = copies.shape[0]
    span_count = copies.shape[1]
    head_count = memory.shape[3]
    flat_rows = copies.reshape(-1, E).astype(jnp.float32)
    normed = rms_rows(flat_rows).astype(jnp.bfloat16)
    enc_query = jnp.dot(normed, query_w, preferred_element_type=jnp.float32).astype(jnp.bfloat16)
    enc_query = enc_query.reshape(groups, span_count, PT, head_count, EHD)
    scores = jnp.einsum(
        "gcqhd,ckhd->gchqk", enc_query, memory[:, :, 0], preferred_element_type=jnp.float32
    ) / math.sqrt(EHD)
    weights = softmax_rows(scores).astype(jnp.bfloat16)
    mixed_heads = jnp.einsum(
        "gchqk,ckhd->gcqhd", weights, memory[:, :, 1], preferred_element_type=jnp.float32
    )
    mixed_heads = mixed_heads.astype(jnp.bfloat16).reshape(-1, head_count * EHD)
    branch = lax.dot_general(
        mixed_heads, out_w, (((1,), (1,)), ((), ())), preferred_element_type=jnp.float32
    )
    return (flat_rows, branch)


def body(
    span_states,
    span_queries,
    span_memory,
    passages,
    neighbours,
    enc_query_w,
    enc_out_w,
    kv_weight,
    out_weight,
):
    device_count = lax.axis_size("span")
    head_index = lax.axis_index("head")
    span_count = neighbours.shape[0]
    owners = neighbours // PS_DEV
    local_ids = neighbours % PS_DEV
    wanted = wanted_slots(owners.reshape(-1), local_ids.reshape(-1), device_count)[:, None]
    fetched = fetch_passages(wanted, passages)
    own_owner = lax.dynamic_index_in_dim(owners, head_index, 1, keepdims=False)
    copies = fetched[own_owner, 0][None]
    query_full, out_full = (
        lax.all_gather(enc_query_w, "head", axis=1, tiled=True),
        lax.all_gather(enc_out_w, "head", axis=1, tiled=True),
    )
    memory_full = lax.all_gather(span_memory, "head", axis=2, tiled=True)
    memory = memory_full.reshape(span_count, CT, 2, -1, EHD)
    own_rows, own_branch = encode_branch(copies, memory, query_full, out_full)
    encoded = rms_rows(own_rows + own_branch).astype(jnp.bfloat16)
    all_encoded = lax.all_gather(encoded[None], "head", axis=0, tiled=True)
    flat_encoded = all_encoded.reshape(-1, E)
    dec_kv = jnp.einsum(
        "re,esc->rsc",
        flat_encoded,
        lax.all_gather(kv_weight, "span", axis=2, tiled=True),
        preferred_element_type=jnp.float32,
    ).astype(jnp.bfloat16)
    head_count = span_queries.shape[1] // HD
    dec_kv = dec_kv.reshape(NB, span_count, PT, 2, head_count, HD)
    dec_query = span_queries.reshape(span_count, CT, head_count, HD)
    scores = jnp.einsum(
        "cqhd,ncphd->chqnp", dec_query, dec_kv[:, :, :, 0], preferred_element_type=jnp.float32
    ) / math.sqrt(HD)
    scores = scores.reshape(span_count, head_count, CT, NB * PT)
    weights = softmax_rows(scores).astype(jnp.bfloat16).reshape(span_count, head_count, CT, NB, PT)
    attended = jnp.einsum(
        "chqnp,ncphd->cqhd", weights, dec_kv[:, :, :, 1], preferred_element_type=jnp.float32
    )
    attended = attended.astype(jnp.bfloat16).reshape(span_count * CT, head_count * HD)
    partial_value = jnp.dot(
        attended,
        lax.all_gather(out_weight, "span", axis=1, tiled=True),
        preferred_element_type=jnp.float32,
    )
    summed = lax.psum_scatter(
        partial_value.astype(jnp.bfloat16), "head", scatter_dimension=1, tiled=True
    ).astype(jnp.float32)
    return (span_states.astype(jnp.float32) + summed).astype(jnp.bfloat16)


def solution(mesh):
    placed = (
        P(("groups", "span"), "head"),
        P(("groups", "span"), "head"),
        P(("groups", "span"), None, "head"),
        P(("groups", "span"), None),
        P(("groups", "span"), None),
        P(None, "head"),
        P(None, "head"),
        P(None, None, ("head", "span")),
        P("head", "span"),
    )
    return jax.shard_map(
        body, mesh=mesh, in_specs=placed, out_specs=P(("groups", "span"), "head"), check_vma=False
    )
```

profile of v0, /device:TPU:0, one launch (start us, length us, event | category | flops | bytes accessed | tf_op | source)
XLA Modules:
  0.0 270.7 jit_solution(14112811568693671814)
XLA Ops:
  6.5 0.0 copy-start
  6.5 0.0 copy-start.4
  6.5 0.0 all-gather.6.cloned.1.call-start
  6.5 0.7 all-gather.6.cloned.1.call-update
  7.3 0.0 all-gather.8.cloned.1.call-start
  7.3 0.7 all-gather.8.cloned.1.call-update
  8.0 0.0 all-gather.10.cloned.1.call-start
  8.1 0.0 copy-done.4
  8.1 0.8 copy.54
  8.9 0.0 all-gather.10.cloned.1.call-update
  8.9 0.0 all-gather.12.cloned.1.call-start
  9.0 0.5 all-gather.12.cloned.1.call-update
  9.5 0.0 copy-done.7
  9.5 0.1 eq.17
  9.6 0.1 broadcast_in_dim.16
  9.7 0.1 select_reduce_fusion
  9.8 0.1 copy.48
  9.9 13.6 %all_to_all.14 = s32[8,1,1]{2,1,0:T(1,128)S(1)} all-to-all(s32[8,1,1]{2,1,0:T(1,128)S(1)} %copy.48), channel_id=1, replica_groups=mesh['groups'=2,'span'=8,'head'=2] {'span'}, dimensions={0} | all-to-all | bytes 64 | tf_op jit(solution)/shard_map/all_to_all | solution.py:34
  23.5 0.2 fusion.20
  23.7 0.0 copy-done
  23.7 2.0 gather_fusion
  25.7 4.4 %all-to-all-start.1 = ((bf16[8,1,128,896]{3,2,1,0:T(8,128)(2,1)}), bf16[8,1,128,896]{3,2,1,0:T(8,128)(2,1)}, u32[]{:S(2)}, u32[]{:S(2)}) async-start(bf16[8,1,128,896]{3,2,1,0:T(8,128)(2,1)} %bitcast.92), calls=%async_computation.1 | async-start | bytes 3670016 | tf_op jit(solution)/shard_map/all_to_all | solution.py:35
  30.2 0.0 reduce-scatter.2.cloned.1.call-start
  30.2 0.0 copy-done.6
  30.2 2.1 all_gather.19
  32.4 0.4 reshape.91
  32.8 1.7 fusion.25
  34.4 1.1 copy.66
  35.5 0.0 copy-done.5
  35.6 0.2 fusion.23
  35.8 0.7 bitcast_bitcast_fusion
  36.5 49.9 %all-to-all-done.1 = bf16[8,1,128,896]{3,2,1,0:T(8,128)(2,1)} async-done(((bf16[8,1,128,896]{3,2,1,0:T(8,128)(2,1)}), bf16[8,1,128,896]{3,2,1,0:T(8,128)(2,1)}, u32[]{:S(2)}, u32[]{:S(2)}) %all-to-all-start.1) | async-done | bytes 1835040 | tf_op jit(solution)/shard_map/all_to_all | solution.py:35
  86.4 2.1 gather_fusion.1
  88.5 0.2 multiply_reduce_fusion.1
  88.7 0.1 fusion.8
  88.8 0.0 all-gather.6.cloned.1.call-done
  88.9 3.0 %convolution_convert_fusion.3 = bf16[256,896]{1,0:T(8,128)(2,1)} fusion(bf16[256,896]{1,0:T(8,128)(2,1)S(1)} %fusion.8, bf16[896,896]{0,1:T(8,128)(2,1)} %all-gather.6.cloned.1.call-done), kind=kOutput, calls=%fused_computation.10 | convolution fusion | flops 411271168 | bytes 2523136 | tf_op jit(solution)/shard_map/dot_general | solution.py:44
  91.9 1.8 reshape.118
  93.7 0.0 copy-start.3
  93.7 1.8 fusion.26
  95.5 0.2 fusion.9
  95.6 0.0 copy-done.3
  95.7 0.3 fusion.2
  96.0 0.5 copy.53
  96.5 0.0 all-gather.8.cloned.1.call-done
  96.5 2.2 multiply_reduce_fusion
  98.8 0.1 multiply_convert_fusion
  98.9 2.5 all-gather
  101.4 23.2 %all-gather.10.cloned.1.call-done = bf16[896,2,1024]{2,0,1:T(8,128)(2,1)} async-done(((bf16[896,2,128]{2,0,1:T(8,128)(2,1)}), bf16[896,2,1024]{2,0,1:T(8,128)(2,1)}) %all-gather.10.cloned.1.call-update) | async-done | bytes 3670032 | tf_op jit(solution)/shard_map/all_gather | solution.py:93
  124.5 4.4 %convolution_convert_fusion.1 = bf16[512,2,1024]{2,0,1:T(8,128)(2,1)S(1)} fusion(bf16[896,2,1024]{2,0,1:T(8,128)(2,1)} %all-gather.10.cloned.1.call-done, bf16[512,896]{1,0:T(8,128)(2,1)S(1)} %all-gather), kind=kOutput, calls=%fused_computation.3 | convolution fusion | flops 1880096768 | bytes 6684672 | tf_op jit(solution)/shard_map/re,esc->rsc/dot_general | solution.py:90
  128.9 0.6 copy.70
  129.5 0.0 copy-start.1
  129.5 0.1 fusion.24
  129.7 0.8 copy-done.1
  130.5 0.6 fusion.27
  131.1 0.4 fusion.5
  131.5 0.5 fusion.4
  132.0 0.2 copy.58
  132.1 117.6 %all-gather.12.cloned.1.call-done = bf16[1024,4096]{1,0:T(8,128)(2,1)} async-done(((bf16[1024,512]{1,0:T(8,128)(2,1)}), bf16[1024,4096]{1,0:T(8,128)(2,1)}) %all-gather.12.cloned.1.call-update) | async-done | bytes 8388624 | tf_op jit(solution)/shard_map/all_gather | solution.py:110
  249.7 5.8 %convolution_convert_fusion = bf16[128,4096]{1,0:T(8,128)(2,1)} fusion(bf16[1024,4096]{1,0:T(8,128)(2,1)} %all-gather.12.cloned.1.call-done, bf16[16,8,8,128]{3,2,1,0:T(8,128)(2,1)S(1)} %bitcast.95), kind=kOutput, calls=%fused_computation.2 | convolution fusion | flops 1074266112 | bytes 9699328 | tf_op jit(solution)/shard_map/dot_general | solution.py:108
  255.5 0.0 reduce-scatter.2.cloned.1.call-update
  255.5 6.7 %reduce-scatter.2.cloned.1.call-done = bf16[128,2048]{1,0:T(8,128)(2,1)} async-done(((bf16[128,4096]{1,0:T(8,128)(2,1)}), bf16[128,2048]{1,0:T(8,128)(2,1)}) %reduce-scatter.2.cloned.1.call-update) | async-done | bytes 524304 | tf_op jit(solution)/shard_map/reduce_scatter | solution.py:113
  262.2 0.0 copy-done.2
  262.2 2.0 add_convert_fusion
  (9 shorter events, 0.1 us)
Async XLA Ops:
  6.5 17.2 %copy-start = (bf16[1024,896]{1,0:T(8,128)(2,1)S(1)}, bf16[1024,896]{1,0:T(8,128)(2,1)}, u32[]{:S(2)}) copy-start(bf16[1024,896]{1,0:T(8,128)(2,1)} %param.12) | copy-start | bytes 5505028
  6.5 1.5 copy-start.4
  6.5 3.0 %copy-start.7 = (s32[2,2]{1,0:T(2,128)S(1)}, s32[2,2]{1,0:T(2,128)}, u32[]{:S(2)}) copy-start(s32[2,2]{1,0:T(2,128)} %param.13) | copy-start | bytes 52
  6.5 82.3 %all-gather.6.cloned.1.call-start = ((), (), s32[]{:S(2)}) async-start(), calls=%async_computation.3 | async-start | bytes 2408448 | tf_op jit(solution)/shard_map/all_gather | solution.py:81
  7.3 89.2 %all-gather.8.cloned.1.call-start = ((), (), s32[]{:S(2)}) async-start(), calls=%async_computation.4 | async-start | bytes 2408448 | tf_op jit(solution)/shard_map/all_gather | solution.py:82
  8.0 116.5 %all-gather.10.cloned.1.call-start = ((), (), s32[]{:S(2)}) async-start(), calls=%async_computation.5 | async-start | bytes 4128768 | tf_op jit(solution)/shard_map/all_gather | solution.py:93
  8.9 240.8 %all-gather.12.cloned.1.call-start = ((), (), s32[]{:S(2)}) async-start(), calls=%async_computation.6 | async-start | bytes 9437184 | tf_op jit(solution)/shard_map/all_gather | solution.py:110
  25.7 4.5 %copy-start.6 = (bf16[128,2,448]{0,2,1:T(8,128)(2,1)S(1)}, bf16[128,2,448]{0,2,1:T(8,128)(2,1)}, u32[]{:S(2)}) copy-start(bf16[128,2,448]{0,2,1:T(8,128)(2,1)} %param.11) | copy-start | bytes 688132
  25.7 60.7 %all-to-all-start.1 = ((bf16[8,1,128,896]{3,2,1,0:T(8,128)(2,1)}), bf16[8,1,128,896]{3,2,1,0:T(8,128)(2,1)}, u32[]{:S(2)}, u32[]{:S(2)}) async-start(bf16[8,1,128,896]{3,2,1,0:T(8,128)(2,1)} %bitcast.92), calls=%async_computation.1 | async-start | bytes 3670016 | tf_op jit(solution)/shard_map/all_to_all | solution.py:35
  30.2 232.1 %reduce-scatter.2.cloned.1.call-start = ((), (), s32[]{:S(2)}) async-start(), calls=%async_computation.7 | async-start | bytes 1572864 | tf_op jit(solution)/shard_map/reduce_scatter | solution.py:113
  32.4 3.2 %copy-start.5 = (bf16[128,1024]{1,0:T(8,128)(2,1)S(1)}, bf16[128,1024]{1,0:T(8,128)(2,1)}, u32[]{:S(2)}) copy-start(bf16[128,1024]{1,0:T(8,128)(2,1)} %param.10) | copy-start | bytes 786436
  93.7 2.0 copy-start.3
  129.5 1.0 copy-start.1
  249.7 12.5 %copy-start.2 = (bf16[128,2048]{1,0:T(8,128)(2,1)S(1)}, bf16[128,2048]{1,0:T(8,128)(2,1)}, u32[]{:S(2)}) copy-start(bf16[128,2048]{1,0:T(8,128)(2,1)} %param.9) | copy-start | bytes 1572868
Sparse Core Ops, SparseCore 0:
  8.9 12.5 all-gather.5
  23.0 11.0 all-gather.7
  36.1 88.3 all-gather.9
  126.4 123.2 all-gather.11
  255.6 6.5 reduce-scatter.1
where the time goes:
time: 271 us
  waiting for transfers between devices  199 us (73%)
  matrix products  18.5 us (7%)
  blocking collectives  18.2 us (7%)
  between operations  13.4 us (5%)
  local copies, waits for them, and re-layouts  13.1 us (5%)
  starting transfers between devices  4.61 us (2%)
  other arithmetic  3.53 us (1%)
    all_gather x1, waiting for transfers between devices, body(): lax.all_gather(out_weight, 'span', axis=1, tiled=True)  118 us
    all_to_all x1, waiting for transfers between devices, fetch_passages(): lax.all_to_all(picked, 'span', split_axis=0, concat_axis=0, tiled=True)  49.9 us
    all_gather x1, waiting for transfers between devices, body(): lax.all_gather(kv_weight, 'span', axis=2, tiled=True)  23.2 us
    all_to_all x1, blocking collectives, fetch_passages(): lax.all_to_all(wanted, 'span', split_axis=0, concat_axis=0, tiled=True)  13.6 us
    reduce_scatter x1, waiting for transfers between devices, body(): lax.psum_scatter(partial_value.astype(jnp.bfloat16), 'head', scatter_dime...  6.73 us
    dot_general x1, matrix products, body(): jnp.dot(attended, lax.all_gather(out_weight, 'span', axis=1, tiled=True),...  5.75 us
  transfers between devices with their start and end apart: 6, of which 4 were waited for; matrix products, arithmetic and copies ran while one was open for 10% of the time, Pallas kernels for 0%

commit v1 on v0

--- a/solution.py
+++ b/solution.py
@@ -12,6 +12,25 @@
 NB = 2
 PS_DEV = 8
 epsilon = 1e-06
+
+
+def joined_along(blocks, dim):
+    blocks = jnp.moveaxis(blocks, 0, dim)
+    lengths = blocks.shape
+    return blocks.reshape(*lengths[:dim], lengths[dim] * lengths[dim + 1], *lengths[dim + 2 :])
+
+
+def work_around(array, axis, dim, work, out_dim):
+    size, position, width = (lax.axis_size(axis), lax.axis_index(axis), array.shape[dim])
+    ahead = [(i, (i + 1) % size) for i in range(size)]
+    blocks = []
+    held = array
+    for hop in range(size):
+        coming = held if hop == size - 1 else lax.ppermute(held, axis, ahead)
+        blocks.append(work(held, (position - hop) % size * width))
+        held = coming
+    blocks = jnp.stack(blocks)[(position - jnp.arange(size)) % size]
+    return joined_along(blocks, out_dim)
 
 
 def rms_rows(values):
@@ -87,11 +106,14 @@
     encoded = rms_rows(own_rows + own_branch).astype(jnp.bfloat16)
     all_encoded = lax.all_gather(encoded[None], "head", axis=0, tiled=True)
     flat_encoded = all_encoded.reshape(-1, E)
-    dec_kv = jnp.einsum(
-        "re,esc->rsc",
-        flat_encoded,
-        lax.all_gather(kv_weight, "span", axis=2, tiled=True),
-        preferred_element_type=jnp.float32,
+    dec_kv = work_around(
+        kv_weight,
+        "span",
+        2,
+        lambda own_block, at: jnp.einsum(
+            "re,esc->rsc", flat_encoded, own_block, preferred_element_type=jnp.float32
+        ),
+        2,
     ).astype(jnp.bfloat16)
     head_count = span_queries.shape[1] // HD
     dec_kv = dec_kv.reshape(NB, span_count, PT, 2, head_count, HD)

time: 271 us -> 294 us (1.085)
  starting transfers between devices: 4.61 us -> 20.7 us
  matrix products: 18.5 us -> 27.5 us
  waiting for transfers between devices: 199 us -> 191 us
  local copies, waits for them, and re-layouts: 13.1 us -> 18.6 us
    ppermute x0 -> x7, waiting for transfers between devices: none -> 159 us  [work_around(): coming = held if hop == size - 1 else lax.ppermute(held, axis, ahead)]
    all_gather x1, waiting for transfers between devices: 118 us -> 0.02 us  [body(): lax.all_gather(out_weight, 'span', axis=1, tiled=True)]
    all_to_all x1, waiting for transfers between devices: 49.9 us -> 0.01 us  [fetch_passages(): lax.all_to_all(picked, 'span', split_axis=0, concat_axis=0, tiled=True)]
    all_gather x1 -> x0, waiting for transfers between devices: 23.2 us -> none  [body(): lax.all_gather(kv_weight, 'span', axis=2, tiled=True)]
    reduce_scatter x1, waiting for transfers between devices: 6.73 us -> 29.5 us  [body(): lax.psum_scatter(partial_value.astype(jnp.bfloat16), 'head', scatter_dime...]
    ppermute x0 -> x7, starting transfers between devices: none -> 16.1 us  [work_around(): coming = held if hop == size - 1 else lax.ppermute(held, axis, ahead)]
    dot_general x1 -> x8, matrix products: 4.37 us -> 13.4 us  [body(): jnp.einsum('re,esc->rsc', flat_encoded, own_block, preferred_element_type...]
    gather x0 -> x1, local copies, waits for them, and re-layouts: none -> 3.72 us  [work_around(): blocks = jnp.stack(blocks)[(position - jnp.arange(size)) % size]]
  transfers between devices with their start and end apart: 6 -> 12, of which waited for: 4 -> 7; matrix products, arithmetic and copies ran while one was open for 10% -> 13% of each run, Pallas kernels for 0% -> 0%
where the time goes in v1:
time: 294 us; the launch traced here: 293 us
  waiting for transfers between devices  191 us (65%)
  matrix products  27.5 us (9%)
  starting transfers between devices  20.7 us (7%)
  local copies, waits for them, and re-layouts  18.6 us (6%)
  blocking collectives  18.5 us (6%)
  between operations  13.4 us (5%)
  other arithmetic  3.54 us (1%)
    ppermute x7, waiting for transfers between devices, work_around(): coming = held if hop == size - 1 else lax.ppermute(held, axis, ahead)  159 us
    reduce_scatter x1, waiting for transfers between devices, body(): lax.psum_scatter(partial_value.astype(jnp.bfloat16), 'head', scatter_dime...  29.5 us
    ppermute x7, starting transfers between devices, work_around(): coming = held if hop == size - 1 else lax.ppermute(held, axis, ahead)  16.1 us
    all_to_all x1, blocking collectives, fetch_passages(): lax.all_to_all(wanted, 'span', split_axis=0, concat_axis=0, tiled=True)  13.6 us
    dot_general x8, matrix products, body(): jnp.einsum('re,esc->rsc', flat_encoded, own_block, preferred_element_type...  13.4 us
  transfers between devices with their start and end apart: 12, of which 7 were waited for; matrix products, arithmetic and copies ran while one was open for 13% of the time, Pallas kernels for 0%

profile of v1, /device:TPU:0, one launch (start us, length us, event | category | flops | bytes accessed | tf_op | source)
XLA Modules:
  0.0 293.3 jit_solution(2058535495606247030)
XLA Ops:
  6.5 0.7 all-gather.5.cloned.1.call-update
  7.3 0.0 all-gather.7.cloned.1.call-start
  7.3 0.7 all-gather.7.cloned.1.call-update
  8.0 0.0 all-gather.9.cloned.1.call-start
  8.1 0.7 all-gather.9.cloned.1.call-update
  8.8 0.1 eq.19
  8.9 0.1 broadcast_in_dim.16
  8.9 0.1 select_reduce_fusion
  9.0 0.1 copy.52
  9.1 13.6 %all_to_all.14 = s32[8,1,1]{2,1,0:T(1,128)S(1)} all-to-all(s32[8,1,1]{2,1,0:T(1,128)S(1)} %copy.52), channel_id=1, replica_groups=mesh['groups'=2,'span'=8,'head'=2] {'span'}, dimensions={0} | all-to-all | bytes 64 | tf_op jit(solution)/shard_map/all_to_all | solution.py:53
  22.7 0.2 fusion.35
  23.0 2.0 gather_fusion
  25.0 4.5 %all-to-all-start.1 = ((bf16[8,1,128,896]{3,2,1,0:T(8,128)(2,1)}), bf16[8,1,128,896]{3,2,1,0:T(8,128)(2,1)}, u32[]{:S(2)}, u32[]{:S(2)}) async-start(bf16[8,1,128,896]{3,2,1,0:T(8,128)(2,1)} %bitcast.143), calls=%async_computation.1 | async-start | bytes 3670016 | tf_op jit(solution)/shard_map/all_to_all | solution.py:54
  29.4 0.0 reduce-scatter.2.cloned.1.call-start
  29.5 0.1 copy.58
  29.6 1.9 collective-permute-start
  31.5 64.0 %collective-permute-done = bf16[896,2,128]{2,0,1:T(8,128)(2,1)S(1)} collective-permute-done((bf16[896,2,128]{2,0,1:T(8,128)(2,1)S(1)}, bf16[896,2,128]{2,0,1:T(8,128)(2,1)S(1)}, u32[]{:S(2)}, u32[]{:S(2)}) %collective-permute-start) | collective-permute-done | bytes 458784 | tf_op jit(solution)/shard_map/ppermute | solution.py:29
  95.5 0.8 copy-done.6
  96.3 22.4 %collective-permute-done.1 = bf16[896,2,128]{2,0,1:T(8,128)(2,1)S(1)} collective-permute-done((bf16[896,2,128]{2,0,1:T(8,128)(2,1)S(1)}, bf16[896,2,128]{2,0,1:T(8,128)(2,1)S(1)}, u32[]{:S(2)}, u32[]{:S(2)}) %collective-permute-start.1) | collective-permute-done | bytes 458784 | tf_op jit(solution)/shard_map/ppermute | solution.py:29
  118.7 0.8 copy-done.8
  119.5 15.0 %collective-permute-done.2 = bf16[896,2,128]{2,0,1:T(8,128)(2,1)S(1)} collective-permute-done((bf16[896,2,128]{2,0,1:T(8,128)(2,1)S(1)}, bf16[896,2,128]{2,0,1:T(8,128)(2,1)S(1)}, u32[]{:S(2)}, u32[]{:S(2)}) %collective-permute-start.2) | collective-permute-done | bytes 458784 | tf_op jit(solution)/shard_map/ppermute | solution.py:29
  134.5 0.8 copy-done.10
  135.2 19.8 %collective-permute-done.3 = bf16[896,2,128]{2,0,1:T(8,128)(2,1)} collective-permute-done((bf16[896,2,128]{2,0,1:T(8,128)(2,1)S(1)}, bf16[896,2,128]{2,0,1:T(8,128)(2,1)}, u32[]{:S(2)}, u32[]{:S(2)}) %collective-permute-start.3) | collective-permute-done | bytes 458784 | tf_op jit(solution)/shard_map/ppermute | solution.py:29
  155.1 2.1 all_gather.16
  157.2 0.4 reshape.141
  157.6 1.7 fusion.43
  159.3 1.1 copy.71
  160.4 0.2 fusion.38
  160.6 16.0 %collective-permute-done.4 = bf16[896,2,128]{2,0,1:T(8,128)(2,1)} collective-permute-done((bf16[896,2,128]{2,0,1:T(8,128)(2,1)}, bf16[896,2,128]{2,0,1:T(8,128)(2,1)}, u32[]{:S(2)}, u32[]{:S(2)}) %collective-permute-start.4) | collective-permute-done | bytes 458784 | tf_op jit(solution)/shard_map/ppermute | solution.py:29
  176.6 0.4 collective-permute-start.5
  177.0 0.7 bitcast_bitcast_fusion
  177.7 22.1 %collective-permute-done.5 = bf16[896,2,128]{2,0,1:T(8,128)(2,1)} collective-permute-done((bf16[896,2,128]{2,0,1:T(8,128)(2,1)}, bf16[896,2,128]{2,0,1:T(8,128)(2,1)}, u32[]{:S(2)}, u32[]{:S(2)}) %collective-permute-start.5) | collective-permute-done | bytes 458784 | tf_op jit(solution)/shard_map/ppermute | solution.py:29
  199.8 13.8 %collective-permute-start.6 = (bf16[896,2,128]{2,0,1:T(8,128)(2,1)}, bf16[896,2,128]{2,0,1:T(8,128)(2,1)}, u32[]{:S(2)}, u32[]{:S(2)}) collective-permute-start(bf16[896,2,128]{2,0,1:T(8,128)(2,1)} %collective-permute-done.5), channel_id=1, source_target_pairs={{0,2},{2,4},{4,6},{6,8},{8,10},{10,12},{12,14},{14,0},{1,3},{3,5},... | collective-permute-start | bytes 1376264 | tf_op jit(solution)/shard_map/ppermute | solution.py:29
  213.6 2.2 gather_fusion.1
  215.8 0.2 multiply_reduce_fusion.1
  216.0 0.1 fusion.23
  216.1 0.0 all-gather.5.cloned.1.call-done
  216.1 3.0 %convolution_convert_fusion.2 = bf16[256,896]{1,0:T(8,128)(2,1)} fusion(bf16[256,896]{1,0:T(8,128)(2,1)S(1)} %fusion.23, bf16[896,896]{0,1:T(8,128)(2,1)} %all-gather.5.cloned.1.call-done), kind=kOutput, calls=%fused_computation.10 | convolution fusion | flops 411271168 | bytes 2523136 | tf_op jit(solution)/shard_map/dot_general | solution.py:63
  219.1 1.8 reshape.175
  220.9 1.8 fusion.44
  222.7 0.2 fusion.24
  222.9 0.3 fusion.10
  223.2 0.5 copy.57
  223.7 0.0 all-gather.7.cloned.1.call-done
  223.7 2.2 multiply_reduce_fusion
  226.0 0.1 multiply_convert_fusion
  226.1 2.8 all-gather
  228.9 1.2 fusion.9
  230.1 1.2 fusion.8
  231.3 1.1 fusion.7
  232.5 1.2 fusion.6
  233.6 2.2 fusion.5
  235.8 2.2 fusion.4
  238.0 2.2 fusion.3
  240.1 2.2 fusion.2
  242.3 3.7 %gather_fusion.2 = bf16[8,512,2,128]{3,1,2,0:T(8,128)(2,1)} fusion(bf16[8,512,2,128]{3,1,2,0:T(8,128)(2,1)} %fusion.2, s32[1024]{0:T(1024)S(1)} %pad_clamp_fusion), kind=kCustom, calls=%fused_computation.2 | custom fusion | bytes 4194336 | tf_op jit(solution)/shard_map/gather | solution.py:32
  246.0 1.7 fusion.42
  247.8 0.6 fusion.45
  248.3 0.4 fusion.13
  248.7 0.5 fusion.12
  249.2 0.2 copy.63
  249.5 5.8 %convolution_convert_fusion = bf16[128,4096]{1,0:T(8,128)(2,1)} fusion(bf16[1024,4096]{1,0:T(8,128)(2,1)} %all-gather.9.cloned.1.call-done, bf16[16,8,8,128]{3,2,1,0:T(8,128)(2,1)S(1)} %bitcast.145), kind=kOutput, calls=%fused_computation.3 | convolution fusion | flops 1074266112 | bytes 9699328 | tf_op jit(solution)/shard_map/dot_general | solution.py:130
  255.2 29.5 %reduce-scatter.2.cloned.1.call-done = bf16[128,2048]{1,0:T(8,128)(2,1)} async-done(((bf16[128,4096]{1,0:T(8,128)(2,1)}), bf16[128,2048]{1,0:T(8,128)(2,1)}) %reduce-scatter.2.cloned.1.call-update) | async-done | bytes 524304 | tf_op jit(solution)/shard_map/reduce_scatter | solution.py:135
  284.8 2.0 add_convert_fusion
  (43 shorter events, 0.2 us)
Async XLA Ops:
  6.5 16.4 %copy-start = (bf16[1024,896]{1,0:T(8,128)(2,1)S(1)}, bf16[1024,896]{1,0:T(8,128)(2,1)}, u32[]{:S(2)}) copy-start(bf16[1024,896]{1,0:T(8,128)(2,1)} %param.12) | copy-start | bytes 5505028
  6.5 2.2 copy-start.14
  6.5 209.6 %all-gather.5.cloned.1.call-start = ((), (), s32[]{:S(2)}) async-start(), calls=%async_computation.3 | async-start | bytes 2408448 | tf_op jit(solution)/shard_map/all_gather | solution.py:100
  7.3 216.5 %all-gather.7.cloned.1.call-start = ((), (), s32[]{:S(2)}) async-start(), calls=%async_computation.4 | async-start | bytes 2408448 | tf_op jit(solution)/shard_map/all_gather | solution.py:101
  8.0 241.4 %all-gather.9.cloned.1.call-start = ((), (), s32[]{:S(2)}) async-start(), calls=%async_computation.5 | async-start | bytes 9437184 | tf_op jit(solution)/shard_map/all_gather | solution.py:132
  25.0 4.5 %copy-start.4 = (bf16[896,2,128]{2,1,0:T(2,128)(2,1)S(1)}, bf16[896,2,128]{2,1,0:T(2,128)(2,1)}, u32[]{:S(2)}) copy-start(bf16[896,2,128]{2,1,0:T(2,128)(2,1)} %param.16) | copy-start | bytes 1376260
  25.0 130.1 %copy-start.13 = (bf16[128,2,448]{0,2,1:T(8,128)(2,1)S(1)}, bf16[128,2,448]{0,2,1:T(8,128)(2,1)}, u32[]{:S(2)}) copy-start(bf16[128,2,448]{0,2,1:T(8,128)(2,1)} %param.11) | copy-start | bytes 688132
  25.0 188.7 %all-to-all-start.1 = ((bf16[8,1,128,896]{3,2,1,0:T(8,128)(2,1)}), bf16[8,1,128,896]{3,2,1,0:T(8,128)(2,1)}, u32[]{:S(2)}, u32[]{:S(2)}) async-start(bf16[8,1,128,896]{3,2,1,0:T(8,128)(2,1)} %bitcast.143), calls=%async_computation.1 | async-start | bytes 3670016 | tf_op jit(solution)/shard_map/all_to_all | solution.py:54
  29.4 255.3 %reduce-scatter.2.cloned.1.call-start = ((), (), s32[]{:S(2)}) async-start(), calls=%async_computation.6 | async-start | bytes 1572864 | tf_op jit(solution)/shard_map/reduce_scatter | solution.py:135
  29.6 65.9 %collective-permute-start = (bf16[896,2,128]{2,0,1:T(8,128)(2,1)S(1)}, bf16[896,2,128]{2,0,1:T(8,128)(2,1)S(1)}, u32[]{:S(2)}, u32[]{:S(2)}) collective-permute-start(bf16[896,2,128]{2,0,1:T(8,128)(2,1)S(1)} %copy.58), channel_id=1, source_target_pairs={{0,2},{2,4},{4,6},{6,8},{8,10},{10,12},{12,14},{14,0},{1,3},{3,5},... | collective-permute-start | bytes 1376264 | tf_op jit(solution)/shard_map/ppermute | solution.py:29
  95.5 0.8 copy-start.6
  96.3 22.4 %collective-permute-start.1 = (bf16[896,2,128]{2,0,1:T(8,128)(2,1)S(1)}, bf16[896,2,128]{2,0,1:T(8,128)(2,1)S(1)}, u32[]{:S(2)}, u32[]{:S(2)}) collective-permute-start(bf16[896,2,128]{2,0,1:T(8,128)(2,1)S(1)} %collective-permute-done), channel_id=1, source_target_pairs={{0,2},{2,4},{4,6},{6,8},{8,10},{10,12},{12,14},{14,0},{1,3},{3,5},... | collective-permute-start | bytes 1376264 | tf_op jit(solution)/shard_map/ppermute | solution.py:29
  118.7 0.8 copy-start.8
  119.5 15.0 %collective-permute-start.2 = (bf16[896,2,128]{2,0,1:T(8,128)(2,1)S(1)}, bf16[896,2,128]{2,0,1:T(8,128)(2,1)S(1)}, u32[]{:S(2)}, u32[]{:S(2)}) collective-permute-start(bf16[896,2,128]{2,0,1:T(8,128)(2,1)S(1)} %collective-permute-done.1), channel_id=1, source_target_pairs={{0,2},{2,4},{4,6},{6,8},{8,10},{10,12},{12,14},{14,0},{1,3},{3,5},... | collective-permute-start | bytes 1376264 | tf_op jit(solution)/shard_map/ppermute | solution.py:29
  134.5 0.8 copy-start.10
  135.2 19.8 %collective-permute-start.3 = (bf16[896,2,128]{2,0,1:T(8,128)(2,1)S(1)}, bf16[896,2,128]{2,0,1:T(8,128)(2,1)}, u32[]{:S(2)}, u32[]{:S(2)}) collective-permute-start(bf16[896,2,128]{2,0,1:T(8,128)(2,1)S(1)} %collective-permute-done.2), channel_id=1, source_target_pairs={{0,2},{2,4},{4,6},{6,8},{8,10},{10,12},{12,14},{14,0},{1,3},{3,5},... | collective-permute-start | bytes 1376264 | tf_op jit(solution)/shard_map/ppermute | solution.py:29
  155.0 21.5 %collective-permute-start.4 = (bf16[896,2,128]{2,0,1:T(8,128)(2,1)}, bf16[896,2,128]{2,0,1:T(8,128)(2,1)}, u32[]{:S(2)}, u32[]{:S(2)}) collective-permute-start(bf16[896,2,128]{2,0,1:T(8,128)(2,1)} %collective-permute-done.3), channel_id=1, source_target_pairs={{0,2},{2,4},{4,6},{6,8},{8,10},{10,12},{12,14},{14,0},{1,3},{3,5},... | collective-permute-start | bytes 1376264 | tf_op jit(solution)/shard_map/ppermute | solution.py:29
  157.2 3.1 %copy-start.12 = (bf16[128,1024]{1,0:T(8,128)(2,1)S(1)}, bf16[128,1024]{1,0:T(8,128)(2,1)}, u32[]{:S(2)}) copy-start(bf16[128,1024]{1,0:T(8,128)(2,1)} %param.10) | copy-start | bytes 786436
  176.6 23.2 %collective-permute-start.5 = (bf16[896,2,128]{2,0,1:T(8,128)(2,1)}, bf16[896,2,128]{2,0,1:T(8,128)(2,1)}, u32[]{:S(2)}, u32[]{:S(2)}) collective-permute-start(bf16[896,2,128]{2,0,1:T(8,128)(2,1)} %collective-permute-done.4), channel_id=1, source_target_pairs={{0,2},{2,4},{4,6},{6,8},{8,10},{10,12},{12,14},{14,0},{1,3},{3,5},... | collective-permute-start | bytes 1376264 | tf_op jit(solution)/shard_map/ppermute | solution.py:29
  199.8 40.3 %collective-permute-start.6 = (bf16[896,2,128]{2,0,1:T(8,128)(2,1)}, bf16[896,2,128]{2,0,1:T(8,128)(2,1)}, u32[]{:S(2)}, u32[]{:S(2)}) collective-permute-start(bf16[896,2,128]{2,0,1:T(8,128)(2,1)} %collective-permute-done.5), channel_id=1, source_target_pairs={{0,2},{2,4},{4,6},{6,8},{8,10},{10,12},{12,14},{14,0},{1,3},{3,5},... | collective-permute-start | bytes 1376264 | tf_op jit(solution)/shard_map/ppermute | solution.py:29
  220.9 2.0 copy-start.3
  226.0 2.9 %copy-start.5 = (bf16[896,2,128]{2,1,0:T(2,128)(2,1)S(1)}, bf16[896,2,128]{2,1,0:T(2,128)(2,1)}, u32[]{:S(2)}) copy-start(bf16[896,2,128]{2,1,0:T(2,128)(2,1)} %param.16) | copy-start | bytes 1376260
  226.0 4.1 %copy-start.7 = (bf16[896,2,128]{2,0,1:T(8,128)(2,1)S(1)}, bf16[896,2,128]{2,0,1:T(8,128)(2,1)}, u32[]{:S(2)}) copy-start(bf16[896,2,128]{2,0,1:T(8,128)(2,1)} %copy-done.6) | copy-start | bytes 1376260
  228.9 2.4 copy-start.9
  230.1 2.3 copy-start.11
  246.0 1.7 copy-start.1
  249.4 35.3 %copy-start.2 = (bf16[128,2048]{1,0:T(8,128)(2,1)S(1)}, bf16[128,2048]{1,0:T(8,128)(2,1)}, u32[]{:S(2)}) copy-start(bf16[128,2048]{1,0:T(8,128)(2,1)} %param.9) | copy-start | bytes 1572868
Sparse Core Ops, SparseCore 0:
  8.9 12.5 all-gather.4
  23.0 11.0 all-gather.6
  36.1 201.6 all-gather.8
  255.4 29.3 reduce-scatter.1
